TPU v7x, 256 devices: a whole 4x4x8 slice. The times are simulated.
256 devices in a mesh: seq: 32 (over x, z), head: 8 (over y, core).
Axes of the slice: x: 4, y: 4, z: 8, core: 2. Of those that a mesh axis runs over, the one named last changes fastest.
Arguments:
- tokens: bfloat16 [16384, 4096], P('seq'), may hold values from -6 to 6
- w_xz: bfloat16 [4096, 2, 4096], P('seq', None, 'head'), may hold values from -0.09375 to 0.09375
- w_bc: bfloat16 [4096, 256], P('seq'), may hold values from -0.09375 to 0.09375
- conv_x: float32 [4, 4096], P(None, 'head'), may hold values from -3 to 3
- conv_bc: float32 [4, 256], replicated, may hold values from -3 to 3
- tail_x: bfloat16 [3, 4096], P(None, 'head'), may hold values from -6 to 6
- tail_bc: bfloat16 [3, 256], replicated, may hold values from -6 to 6
- decay_code: int32 [16384, 64], P('seq', 'head'), may hold values from 0 to 196608, as said below
- skip_gain: float32 [64], P('head'), may hold values from 0.5 to 2
- state_in: float32 [64, 64, 128], P('head'), may hold values from -180 to 180
- norm_gain: float32 [4096], P('head'), may hold values from 0.1 to 1.9
- w_out: bfloat16 [4096, 4096], P('head', 'seq'), may hold values from -0.1875 to 0.1875
Outputs:
- mixed: bfloat16 [16384, 4096], P('seq', 'head')
Inputs may be any that keep to these rules, and one draw needn't show every extreme that they name: `decay_code`: the decay factor of a token and head is exp(-code / 262144).
All inputs are finite; a program needn't handle non-finite values.
Results may differ from a plain program's by a relative error of at most 0.0085.
Values may be sent and summed in bfloat16 or wider, within the bound.
A program may use at most 128 MiB of HBM per device.

v0:
```python
import jax
import jax.numpy as jnp
from jax import lax
from jax.sharding import PartitionSpec as P

Q = 256


def passed_along(value, axis, by):
    size = lax.axis_size(axis)
    pairs = [(i, i + by) for i in range(size) if 0 <= i + by < size]
    return lax.ppermute(value, axis, pairs)


def depthwise(pre, tail, kernel):
    whole = jnp.concatenate([tail, pre], axis=0).astype(jnp.float32)
    length = pre.shape[0]
    total = jnp.zeros((length, pre.shape[1]), jnp.float32)
    for offset in range(kernel.shape[0]):
        total = total + kernel[offset] * whole[offset : offset + length]
    return jax.nn.silu(total).astype(jnp.bfloat16)


def entering_state(decay, end_state, state_in):
    count = lax.axis_size("seq")
    me = lax.axis_index("seq")
    first = me == 0
    got_a, got_s = passed_along((decay, end_state), "seq", 1)
    acc_a = jnp.where(first, jnp.zeros_like(decay), got_a)
    acc_s = jnp.where(first, state_in, got_s)
    step = 1
    while step < count:
        far_a, far_s = passed_along((acc_a, acc_s), "seq", step)
        has = me >= step
        acc_s = jnp.where(has, acc_a[:, None, None] * far_s + acc_s, acc_s)
        acc_a = jnp.where(has, acc_a * far_a, acc_a)
        step *= 2
    return acc_s


def local(
    tokens,
    w_xz,
    w_bc,
    conv_x,
    conv_bc,
    tail_x,
    tail_bc,
    decay_code,
    skip_gain,
    state_in,
    norm_gain,
    w_out,
):
    rows = tokens.shape[0]
    heads, head_dim, nstate = state_in.shape
    inner = heads * head_dim
    seq_count = lax.axis_size("seq")
    first = lax.axis_index("seq") == 0
    pieces = (
        lax.all_gather(w_xz, "seq", axis=0, tiled=True),
        lax.all_gather(w_bc, "seq", axis=0, tiled=True),
    )
    count = pieces[0].shape[0]
    xz = jnp.dot(tokens, pieces[0].reshape(count, 2 * inner), preferred_element_type=jnp.float32)
    bc_sum = jnp.dot(tokens, pieces[1], preferred_element_type=jnp.float32)
    x_pre = xz[:, :inner].astype(jnp.bfloat16)
    z_val = xz[:, inner:].astype(jnp.bfloat16)
    bc_pre = bc_sum.astype(jnp.bfloat16)
    lag = conv_x.shape[0] - 1
    before_x, before_bc = passed_along((x_pre[rows - lag :], bc_pre[rows - lag :]), "seq", 1)
    before_x = jnp.where(first, tail_x, before_x)
    before_bc = jnp.where(first, tail_bc, before_bc)
    x_conv = depthwise(x_pre, before_x, conv_x)
    bc_conv = depthwise(bc_pre, before_bc, conv_bc)
    b_val = bc_conv[:, :nstate]
    c_val = bc_conv[:, nstate:]
    logdec = -decay_code.astype(jnp.float32) / (16.0 * rows * seq_count)
    blocks = rows // Q
    xb = x_conv.reshape(blocks, Q, heads, head_dim)
    bb = b_val.reshape(blocks, Q, nstate)
    cb = c_val.reshape(blocks, Q, nstate)
    cum = jnp.cumsum(logdec.reshape(blocks, Q, heads), axis=1)
    tail_decay = jnp.exp(cum[:, -1:, :] - cum)
    decayed_b = (
        jnp.transpose(tail_decay, (0, 2, 1))[..., None] * bb.astype(jnp.float32)[:, None]
    ).astype(jnp.bfloat16)
    added = jnp.einsum("bhsn,bshp->bhpn", decayed_b, xb, preferred_element_type=jnp.float32)
    block_decay = jnp.exp(cum[:, -1, :])
    before = [None]
    running = added[0]
    for b in range(1, blocks):
        before.append(running)
        running = block_decay[b][:, None, None] * running + added[b]
    cum_range = jnp.cumsum(logdec, axis=0)
    range_decay = jnp.exp(cum_range[-1])
    incoming = entering_state(range_decay, running, state_in)
    places = jnp.arange(Q)
    lower = places[:, None] >= places[None, :]
    cumt = jnp.transpose(cum, (0, 2, 1))
    diff = cumt[:, :, :, None] - cumt[:, :, None, :]
    decay = jnp.where(lower, jnp.exp(jnp.where(lower, diff, 0.0)), 0.0)
    scores = jnp.einsum("btn,bsn->bts", cb, bb, preferred_element_type=jnp.float32)
    weights = (decay * scores[:, None]).astype(jnp.bfloat16)
    parts = jnp.einsum("bhts,bshp->bthp", weights, xb, preferred_element_type=jnp.float32)
    pieces_out = [parts[0]]
    for b in range(1, blocks):
        carried = jnp.einsum(
            "tn,hpn->thp", cb[b].astype(jnp.float32), before[b], precision=lax.Precision.HIGHEST
        )
        pieces_out.append(parts[b] + carried * jnp.exp(cum[b])[:, :, None])
    parts = jnp.concatenate(pieces_out, axis=0)
    correction = jnp.einsum(
        "tn,hpn->thp", c_val.astype(jnp.float32), incoming, precision=lax.Precision.HIGHEST
    )
    parts = (parts + correction * jnp.exp(cum_range)[:, :, None]).reshape(rows, inner)
    y_val = parts / nstate + jnp.repeat(skip_gain, head_dim)[None, :] * x_conv.astype(jnp.float32)
    gated = y_val * jax.nn.silu(z_val.astype(jnp.float32))
    total_sq = lax.psum(jnp.sum(gated * gated, axis=1), "head")
    meansq = total_sq / (inner * lax.axis_size("head"))
    normed = (gated * lax.rsqrt(meansq[:, None] + 1e-05) * norm_gain[None, :]).astype(jnp.bfloat16)
    partial_out = jnp.dot(
        normed, lax.all_gather(w_out, "seq", axis=1, tiled=True), preferred_element_type=jnp.float32
    )
    result = lax.psum_scatter(partial_out, "head", scatter_dimension=1, tiled=True)
    return result.astype(jnp.bfloat16)


def solution(mesh):
    return jax.shard_map(
        local,
        mesh=mesh,
        in_specs=(
            P("seq", None),
            P("seq", None, "head"),
            P("seq", None),
            P(None, "head"),
            P(),
            P(None, "head"),
            P(),
            P("seq", "head"),
            P("head"),
            P("head", None, None),
            P("head"),
            P("head", "seq"),
        ),
        out_specs=P("seq", "head"),
        check_vma=False,
    )
```

profile of v0, /device:TPU:1, one launch (start us, length us, event | category | flops | bytes accessed | tf_op | source)
XLA Modules:
  0.0 390.6 jit_solution(13135936368089963105)
XLA Ops:
  8.8 1.1 reduce-window.16
  11.6 4.9 %collective-permute-start.2 = (f32[8]{0:T(128)}, f32[8]{0:T(128)}, u32[]{:S(2)}, u32[]{:S(2)}) collective-permute-start(f32[8]{0:T(128)} %fusion.32), channel_id=1, source_target_pairs={{0,8},{8,16},{16,24},{24,32},{32,40},{40,48},{48,56},{56,64},{64,7... | collective-permute-start | bytes 104 | tf_op jit(solution)/shard_map/ppermute | solution.py:12
  16.6 1.2 reduce-window.14
  20.6 67.2 %all-gather.6.cloned.1.call-done = bf16[4096,256]{1,0:T(8,128)(2,1)} async-done(((bf16[128,256]{1,0:T(8,128)(2,1)}), bf16[4096,256]{1,0:T(8,128)(2,1)}) %all-gather.6.cloned.1.call-update) | async-done | bytes 2097168 | tf_op jit(solution)/shard_map/all_gather | solution.py:62
  87.8 4.1 %convolution_convert_fusion.1 = bf16[512,256]{1,0:T(8,128)(2,1)S(1)} fusion(bf16[512,4096]{1,0:T(8,128)(2,1)} %param.12, bf16[4096,256]{1,0:T(8,128)(2,1)} %all-gather.6.cloned.1.call-done), kind=kOutput, calls=%fused_computation.17 | convolution fusion | flops 1073872896 | bytes 6553600 | tf_op jit(solution)/shard_map/dot_general | solution.py:66
  91.9 2.4 collective-permute-start.1
  95.5 93.9 %all-gather.4.cloned.1.call-done = bf16[4096,2,512]{2,1,0:T(2,128)(2,1)} async-done(((bf16[128,2,512]{2,1,0:T(2,128)(2,1)}), bf16[4096,2,512]{2,1,0:T(2,128)(2,1)}) %all-gather.4.cloned.1.call-update) | async-done | bytes 8388624 | tf_op jit(solution)/shard_map/all_gather | solution.py:61
  189.4 9.3 %copy.35 = bf16[512,8,2,512]{3,1,2,0:T(8,128)(2,1)} copy(bf16[512,8,2,512]{3,2,1,0:T(2,128)(2,1)} %bitcast.69) | data formatting | bytes 16777216
  198.7 9.3 %convolution_convert_fusion = bf16[512,1024]{1,0:T(8,128)(2,1)S(1)} fusion(bf16[512,4096]{1,0:T(8,128)(2,1)} %param.12, bf16[4096,1024]{1,0:T(8,128)(2,1)} %bitcast.70), kind=kOutput, calls=%fused_computation.8 | convolution fusion | flops 4295491584 | bytes 13631488 | tf_op jit(solution)/shard_map/dot_general | solution.py:65
  208.1 1.3 collective-permute-start
  212.8 1.9 fusion.14
  215.4 3.8 collective-permute-start.7
  220.8 4.5 %collective-permute-done.7 = f32[8,64,128]{2,1,0:T(8,128)S(1)} collective-permute-done((f32[8,64,128]{2,1,0:T(8,128)S(1)}, f32[8,64,128]{2,1,0:T(8,128)S(1)}, u32[]{:S(2)}, u32[]{:S(2)}) %collective-permute-start.7) | collective-permute-done | bytes 262176 | tf_op jit(solution)/shard_map/ppermute | solution.py:12
  226.2 3.3 collective-permute-start.8
  229.5 3.2 collective-permute-start.3
  233.5 5.8 %collective-permute-start.4 = (f32[8]{0:T(128)S(1)}, f32[8]{0:T(128)S(1)}, u32[]{:S(2)}, u32[]{:S(2)}) collective-permute-start(f32[8]{0:T(128)S(1)} %broadcast_select_fusion.4), channel_id=1, source_target_pairs={{0,16},{8,24},{16,32},{24,40},{32,48},{40,56},{48,64},{56,72},{64,... | collective-permute-start | bytes 104 | tf_op jit(solution)/shard_map/ppermute | solution.py:12
  239.5 4.8 %collective-permute-start.9 = (f32[8,64,128]{2,1,0:T(8,128)S(1)}, f32[8,64,128]{2,1,0:T(8,128)S(1)}, u32[]{:S(2)}, u32[]{:S(2)}) collective-permute-start(f32[8,64,128]{2,1,0:T(8,128)S(1)} %add_select_fusion.4), channel_id=1, source_target_pairs={{0,16},{8,24},{16,32},{24,40},{32,48},{40,56},{48,64},{56,72},{64,... | collective-permute-start | bytes 786440 | tf_op jit(solution)/shard_map/ppermute | solution.py:12
  244.3 6.0 %collective-permute-start.5 = (f32[8]{0:T(128)S(1)}, f32[8]{0:T(128)S(1)}, u32[]{:S(2)}, u32[]{:S(2)}) collective-permute-start(f32[8]{0:T(128)S(1)} %broadcast_select_fusion.5), channel_id=1, source_target_pairs={{0,32},{8,40},{16,48},{24,56},{32,64},{40,72},{48,80},{56,88},{64,... | collective-permute-start | bytes 104 | tf_op jit(solution)/shard_map/ppermute | solution.py:12
  250.4 7.9 %collective-permute-done.5 = f32[8]{0:T(128)S(1)} collective-permute-done((f32[8]{0:T(128)S(1)}, f32[8]{0:T(128)S(1)}, u32[]{:S(2)}, u32[]{:S(2)}) %collective-permute-start.5) | collective-permute-done | bytes 64 | tf_op jit(solution)/shard_map/ppermute | solution.py:12
  258.2 9.1 %collective-permute-start.6 = (f32[8]{0:T(128)S(1)}, f32[8]{0:T(128)S(1)}, u32[]{:S(2)}, u32[]{:S(2)}) collective-permute-start(f32[8]{0:T(128)S(1)} %broadcast_select_fusion.6), channel_id=1, source_target_pairs={{0,64},{8,72},{16,80},{24,88},{32,96},{40,104},{48,112},{56,120},{... | collective-permute-start | bytes 104 | tf_op jit(solution)/shard_map/ppermute | solution.py:12
  267.5 1.3 collective-permute-start.10
  269.9 9.3 %collective-permute-done.10 = f32[8,64,128]{2,1,0:T(8,128)S(1)} collective-permute-done((f32[8,64,128]{2,1,0:T(8,128)S(1)}, f32[8,64,128]{2,1,0:T(8,128)S(1)}, u32[]{:S(2)}, u32[]{:S(2)}) %collective-permute-start.10) | collective-permute-done | bytes 262176 | tf_op jit(solution)/shard_map/ppermute | solution.py:12
  279.3 4.5 %collective-permute-start.11 = (f32[8,64,128]{2,1,0:T(8,128)S(1)}, f32[8,64,128]{2,1,0:T(8,128)S(1)}, u32[]{:S(2)}, u32[]{:S(2)}) collective-permute-start(f32[8,64,128]{2,1,0:T(8,128)S(1)} %add_select_fusion.2), channel_id=1, source_target_pairs={{0,64},{8,72},{16,80},{24,88},{32,96},{40,104},{48,112},{56,120},{... | collective-permute-start | bytes 786440 | tf_op jit(solution)/shard_map/ppermute | solution.py:12
  283.9 1.3 fusion.6
  285.2 2.2 collective-permute-done.11
  287.5 6.9 %collective-permute-start.12 = (f32[8,64,128]{2,1,0:T(8,128)S(1)}, f32[8,64,128]{2,1,0:T(8,128)S(1)}, u32[]{:S(2)}, u32[]{:S(2)}) collective-permute-start(f32[8,64,128]{2,1,0:T(8,128)S(1)} %add_select_fusion.1), channel_id=1, source_target_pairs={{0,128},{8,136},{16,144},{24,152},{32,160},{40,168},{48,176},{56,1... | collective-permute-start | bytes 786440 | tf_op jit(solution)/shard_map/ppermute | solution.py:12
  294.9 2.8 collective-permute-done.12
  298.8 2.1 multiply_reduce_fusion
  301.0 16.9 %psum.7 = f32[512]{0:T(512)S(1)} all-reduce(f32[512]{0:T(512)S(1)} %get-tuple-element.5), channel_id=1, replica_groups=mesh['seq'=32,'head'=8] {'head'}, use_global_device_ids=true, to_apply=%region_5.6 | all-reduce | flops 512 | bytes 4096 | tf_op jit(solution)/shard_map/psum | solution.py:119
  317.9 7.8 %fusion.20 = f32[512,4096]{1,0:T(8,128)} fusion(bf16[512,4096]{1,0:T(8,128)(2,1)} %all-gather.8.cloned.1.call-done, f32[512,512]{1,0:T(8,128)S(1)} %get-tuple-element.6, f32[512]{0:T(512)S(1)} %copy-done.3, f32[512]{0:T(512)S(1)} %add_rsqrt_fusion), kind=kOutput, calls=%fused_computation.36 | convolution fusion | flops 2148270080 | bytes 13635584 | tf_op jit(solution)/shard_map/dot_general | solution.py:122
  325.7 56.2 %reduce-scatter.2.cloned.1.call-done = f32[512,512]{1,0:T(8,128)} async-done(((f32[512,4096]{1,0:T(8,128)}), f32[512,512]{1,0:T(8,128)}) %reduce-scatter.2.cloned.1.call-update) | async-done | bytes 1048592 | tf_op jit(solution)/shard_map/reduce_scatter | solution.py:125
  381.9 2.1 convert_element_type.59
  (97 shorter events, 18.2 us)
Async XLA Ops:
  6.5 81.2 %all-gather.6.cloned.1.call-start = ((), (), s32[]{:S(2)}) async-start(), calls=%async_computation.2 | async-start | bytes 2162688 | tf_op jit(solution)/shard_map/all_gather | solution.py:62
  7.3 182.1 %all-gather.4.cloned.1.call-start = ((), (), s32[]{:S(2)}) async-start(), calls=%async_computation.1 | async-start | bytes 8650752 | tf_op jit(solution)/shard_map/all_gather | solution.py:61
  8.0 87.1 %copy-start.14 = (bf16[3,256]{1,0:T(4,128)(2,1)S(1)}, bf16[3,256]{1,0:T(4,128)(2,1)}, u32[]{:S(2)}) copy-start(bf16[3,256]{1,0:T(4,128)(2,1)} %param.18) | copy-start | bytes 4612
  8.0 309.9 %all-gather.8.cloned.1.call-start = ((), (), s32[]{:S(2)}) async-start(), calls=%async_computation.3 | async-start | bytes 4325376 | tf_op jit(solution)/shard_map/all_gather | solution.py:123
  11.6 218.0 %collective-permute-start.2 = (f32[8]{0:T(128)}, f32[8]{0:T(128)}, u32[]{:S(2)}, u32[]{:S(2)}) collective-permute-start(f32[8]{0:T(128)} %fusion.32), channel_id=1, source_target_pairs={{0,8},{8,16},{16,24},{24,32},{32,40},{40,48},{48,56},{56,64},{64,7... | collective-permute-start | bytes 104 | tf_op jit(solution)/shard_map/ppermute | solution.py:12
  16.5 365.4 %reduce-scatter.2.cloned.1.call-start = ((), (), s32[]{:S(2)}) async-start(), calls=%async_computation.4 | async-start | bytes 9437184 | tf_op jit(solution)/shard_map/reduce_scatter | solution.py:125
  18.0 0.8 copy-start.2
  19.7 191.3 %copy-start.4 = (f32[1,512]{1,0:T(1,128)}, f32[1,512]{1,0:T(1,128)S(1)}, u32[]{:S(2)}) copy-start(f32[1,512]{1,0:T(1,128)S(1)} %get-tuple-element.15) | copy-start | bytes 6148
  19.7 191.3 %copy-start.6 = (f32[1,512]{1,0:T(1,128)}, f32[1,512]{1,0:T(1,128)S(1)}, u32[]{:S(2)}) copy-start(f32[1,512]{1,0:T(1,128)S(1)} %get-tuple-element.16) | copy-start | bytes 6148
  19.7 191.3 %copy-start.8 = (f32[1,512]{1,0:T(1,128)}, f32[1,512]{1,0:T(1,128)S(1)}, u32[]{:S(2)}) copy-start(f32[1,512]{1,0:T(1,128)S(1)} %get-tuple-element.17) | copy-start | bytes 6148
  19.7 191.3 %copy-start.10 = (f32[1,512]{1,0:T(1,128)}, f32[1,512]{1,0:T(1,128)S(1)}, u32[]{:S(2)}) copy-start(f32[1,512]{1,0:T(1,128)S(1)} %get-tuple-element.18) | copy-start | bytes 6148
  91.9 3.2 collective-permute-start.1
  198.7 12.1 %copy-start.13 = (bf16[3,512]{1,0:T(4,128)(2,1)S(1)}, bf16[3,512]{1,0:T(4,128)(2,1)}, u32[]{:S(2)}) copy-start(bf16[3,512]{1,0:T(4,128)(2,1)} %param.17) | copy-start | bytes 9220
  208.0 2.8 copy-start
  208.1 2.7 collective-permute-start
  212.8 71.1 %copy-start.12 = (f32[2,8,256]{2,1,0:T(8,128)S(1)}, f32[2,8,256]{2,1,0:T(8,128)}, u32[]{:S(2)}) copy-start(f32[2,8,256]{2,1,0:T(8,128)} %get-tuple-element.10) | copy-start | bytes 49156
  215.4 9.8 %collective-permute-start.7 = (f32[8,64,128]{2,1,0:T(8,128)S(1)}, f32[8,64,128]{2,1,0:T(8,128)S(1)}, u32[]{:S(2)}, u32[]{:S(2)}) collective-permute-start(f32[8,64,128]{2,1,0:T(8,128)S(1)} %fusion.26), channel_id=1, source_target_pairs={{0,8},{8,16},{16,24},{24,32},{32,40},{40,48},{48,56},{56,64},{64,7... | collective-permute-start | bytes 786440 | tf_op jit(solution)/shard_map/ppermute | solution.py:12
  226.2 13.1 %collective-permute-start.8 = (f32[8,64,128]{2,1,0:T(8,128)S(1)}, f32[8,64,128]{2,1,0:T(8,128)S(1)}, u32[]{:S(2)}, u32[]{:S(2)}) collective-permute-start(f32[8,64,128]{2,1,0:T(8,128)S(1)} %broadcast_select_fusion), channel_id=1, source_target_pairs={{0,8},{8,16},{16,24},{24,32},{32,40},{40,48},{48,56},{56,64},{64,7... | collective-permute-start | bytes 786440 | tf_op jit(solution)/shard_map/ppermute | solution.py:12
  229.5 3.9 %collective-permute-start.3 = (f32[8]{0:T(128)S(1)}, f32[8]{0:T(128)S(1)}, u32[]{:S(2)}, u32[]{:S(2)}) collective-permute-start(f32[8]{0:T(128)S(1)} %broadcast_select_fusion.3), channel_id=1, source_target_pairs={{0,8},{8,16},{16,24},{24,32},{32,40},{40,48},{48,56},{56,64},{64,7... | collective-permute-start | bytes 104 | tf_op jit(solution)/shard_map/ppermute | solution.py:12
  233.5 10.8 %collective-permute-start.4 = (f32[8]{0:T(128)S(1)}, f32[8]{0:T(128)S(1)}, u32[]{:S(2)}, u32[]{:S(2)}) collective-permute-start(f32[8]{0:T(128)S(1)} %broadcast_select_fusion.4), channel_id=1, source_target_pairs={{0,16},{8,24},{16,32},{24,40},{32,48},{40,56},{48,64},{56,72},{64,... | collective-permute-start | bytes 104 | tf_op jit(solution)/shard_map/ppermute | solution.py:12
  239.5 27.9 %collective-permute-start.9 = (f32[8,64,128]{2,1,0:T(8,128)S(1)}, f32[8,64,128]{2,1,0:T(8,128)S(1)}, u32[]{:S(2)}, u32[]{:S(2)}) collective-permute-start(f32[8,64,128]{2,1,0:T(8,128)S(1)} %add_select_fusion.4), channel_id=1, source_target_pairs={{0,16},{8,24},{16,32},{24,40},{32,48},{40,56},{48,64},{56,72},{64,... | collective-permute-start | bytes 786440 | tf_op jit(solution)/shard_map/ppermute | solution.py:12
  244.3 13.9 %collective-permute-start.5 = (f32[8]{0:T(128)S(1)}, f32[8]{0:T(128)S(1)}, u32[]{:S(2)}, u32[]{:S(2)}) collective-permute-start(f32[8]{0:T(128)S(1)} %broadcast_select_fusion.5), channel_id=1, source_target_pairs={{0,32},{8,40},{16,48},{24,56},{32,64},{40,72},{48,80},{56,88},{64,... | collective-permute-start | bytes 104 | tf_op jit(solution)/shard_map/ppermute | solution.py:12
  258.2 10.6 %collective-permute-start.6 = (f32[8]{0:T(128)S(1)}, f32[8]{0:T(128)S(1)}, u32[]{:S(2)}, u32[]{:S(2)}) collective-permute-start(f32[8]{0:T(128)S(1)} %broadcast_select_fusion.6), channel_id=1, source_target_pairs={{0,64},{8,72},{16,80},{24,88},{32,96},{40,104},{48,112},{56,120},{... | collective-permute-start | bytes 104 | tf_op jit(solution)/shard_map/ppermute | solution.py:12
  267.5 11.8 %collective-permute-start.10 = (f32[8,64,128]{2,1,0:T(8,128)S(1)}, f32[8,64,128]{2,1,0:T(8,128)S(1)}, u32[]{:S(2)}, u32[]{:S(2)}) collective-permute-start(f32[8,64,128]{2,1,0:T(8,128)S(1)} %add_select_fusion.3), channel_id=1, source_target_pairs={{0,32},{8,40},{16,48},{24,56},{32,64},{40,72},{48,80},{56,88},{64,... | collective-permute-start | bytes 786440 | tf_op jit(solution)/shard_map/ppermute | solution.py:12
  279.3 8.1 %collective-permute-start.11 = (f32[8,64,128]{2,1,0:T(8,128)S(1)}, f32[8,64,128]{2,1,0:T(8,128)S(1)}, u32[]{:S(2)}, u32[]{:S(2)}) collective-permute-start(f32[8,64,128]{2,1,0:T(8,128)S(1)} %add_select_fusion.2), channel_id=1, source_target_pairs={{0,64},{8,72},{16,80},{24,88},{32,96},{40,104},{48,112},{56,120},{... | collective-permute-start | bytes 786440 | tf_op jit(solution)/shard_map/ppermute | solution.py:12
  283.9 13.9 %copy-start.1 = (f32[512,8]{0,1:T(8,128)S(1)}, f32[512,8]{0,1:T(8,128)}, u32[]{:S(2)}) copy-start(f32[512,8]{0,1:T(8,128)} %get-tuple-element.7) | copy-start | bytes 49156
  285.1 13.7 %copy-start.5 = (f32[1,512]{1,0:T(1,128)S(1)}, f32[1,512]{1,0:T(1,128)}, u32[]{:S(2)}) copy-start(f32[1,512]{1,0:T(1,128)} %copy-done.4) | copy-start | bytes 6148
  285.1 13.7 %copy-start.7 = (f32[1,512]{1,0:T(1,128)S(1)}, f32[1,512]{1,0:T(1,128)}, u32[]{:S(2)}) copy-start(f32[1,512]{1,0:T(1,128)} %copy-done.6) | copy-start | bytes 6148
  285.2 13.7 %copy-start.9 = (f32[1,512]{1,0:T(1,128)S(1)}, f32[1,512]{1,0:T(1,128)}, u32[]{:S(2)}) copy-start(f32[1,512]{1,0:T(1,128)} %copy-done.8) | copy-start | bytes 6148
  285.2 13.7 %copy-start.11 = (f32[1,512]{1,0:T(1,128)S(1)}, f32[1,512]{1,0:T(1,128)}, u32[]{:S(2)}) copy-start(f32[1,512]{1,0:T(1,128)} %copy-done.10) | copy-start | bytes 6148
  287.5 10.2 %collective-permute-start.12 = (f32[8,64,128]{2,1,0:T(8,128)S(1)}, f32[8,64,128]{2,1,0:T(8,128)S(1)}, u32[]{:S(2)}, u32[]{:S(2)}) collective-permute-start(f32[8,64,128]{2,1,0:T(8,128)S(1)} %add_select_fusion.1), channel_id=1, source_target_pairs={{0,128},{8,136},{16,144},{24,152},{32,160},{40,168},{48,176},{56,1... | collective-permute-start | bytes 786440 | tf_op jit(solution)/shard_map/ppermute | solution.py:12
  298.4 19.4 %copy-start.3 = (f32[512]{0:T(512)S(1)}, f32[512]{0:T(512)}, u32[]{:S(2)}) copy-start(f32[512]{0:T(512)} %param.22) | copy-start | bytes 6148
Sparse Core Ops, SparseCore 0:
  9.9 77.7 all-gather.5
  90.4 98.9 all-gather.3
  191.9 97.9 all-gather.7
  325.8 56.0 reduce-scatter.1
where the time goes:
time: 391 us
  waiting for transfers between devices  246 us (63%)
  starting transfers between devices  57.6 us (15%)
  matrix products  26.6 us (7%)
  blocking collectives  16.9 us (4%)
  local copies, waits for them, and re-layouts  16.5 us (4%)
  between operations  13.7 us (4%)
  other arithmetic  12.8 us (3%)
    all_gather x1, waiting for transfers between devices, local(): lax.all_gather(w_xz, 'seq', axis=0, tiled=True)  93.9 us
    all_gather x1, waiting for transfers between devices, local(): lax.all_gather(w_bc, 'seq', axis=0, tiled=True)  67.2 us
    ppermute x13, starting transfers between devices, passed_along(): return lax.ppermute(value, axis, pairs)  57.5 us
    reduce_scatter x1, waiting for transfers between devices, local(): lax.psum_scatter(partial_out, 'head', scatter_dimension=1, tiled=True)  56.2 us
    ppermute x13, waiting for transfers between devices, passed_along(): return lax.ppermute(value, axis, pairs)  27.7 us
    psum x1, blocking collectives, local(): total_sq = lax.psum(jnp.sum(gated * gated, axis=1), 'head')  16.9 us
    unnamed x31, local copies, waits for them, and re-layouts  9.4 us
    dot_general x1, matrix products, local(): jnp.dot(tokens, pieces[0].reshape(count, 2 * inner), preferred_element_ty...  9.3 us
  transfers between devices with their start and end apart: 17, of which 10 were waited for; matrix products, arithmetic and copies ran while one was open for 12% of the time, Pallas kernels for 0%

commit v1 on v0

--- a/solution.py
+++ b/solution.py
@@ -58,7 +58,9 @@
     seq_count = lax.axis_size("seq")
     first = lax.axis_index("seq") == 0
     pieces = (
-        lax.all_gather(w_xz, "seq", axis=0, tiled=True),
+        jnp.concatenate(
+            lax.all_to_all(jnp.stack([w_xz] * lax.axis_size("seq")), "seq", 0, 0), axis=0
+        ),
         lax.all_gather(w_bc, "seq", axis=0, tiled=True),
     )
     count = pieces[0].shape[0]

time: 391 us -> 435 us (1.11)
  starting transfers between devices: 57.6 us -> 81.6 us
  waiting for transfers between devices: 246 us -> 256 us
  local copies, waits for them, and re-layouts: 16.5 us -> 25.1 us
    all_gather x1 -> x0, waiting for transfers between devices: 93.9 us -> none  [local(): lax.all_gather(w_xz, 'seq', axis=0, tiled=True)]
    ppermute x13, waiting for transfers between devices: 27.7 us -> 93.1 us  [passed_along(): return lax.ppermute(value, axis, pairs)]
    all_gather x1, waiting for transfers between devices: 67.2 us -> 111 us  [local(): lax.all_gather(w_bc, 'seq', axis=0, tiled=True)]
    all_to_all x0 -> x1, starting transfers between devices: none -> 12.1 us  [local(): lax.all_to_all(jnp.stack([w_xz] * lax.axis_size('seq')), 'seq', 0, 0)]
    ppermute x13, starting transfers between devices: 57.5 us -> 69.3 us  [passed_along(): return lax.ppermute(value, axis, pairs)]
    another operation x3 -> x4, local copies, waits for them, and re-layouts: 0.17 us -> 9.69 us  [the longest x1 9.52 us: local(): jnp.stack([w_xz] * lax.axis_size('seq'))]
    reduce_scatter x1, waiting for transfers between devices: 56.2 us -> 50.7 us  [local(): lax.psum_scatter(partial_out, 'head', scatter_dimension=1, tiled=True)]
    unnamed x31 -> x37, local copies, waits for them, and re-layouts: 9.4 us -> 10 us
  transfers between devices with their start and end apart: 17 -> 17, of which waited for: 10 -> 9; matrix products, arithmetic and copies ran while one was open for 12% -> 10% of each run, Pallas kernels for 0% -> 0%
where the time goes in v1:
time: 435 us; the launch traced here: 434 us
  waiting for transfers between devices  256 us (59%)
  starting transfers between devices  81.6 us (19%)
  matrix products  26.5 us (6%)
  local copies, waits for them, and re-layouts  25.1 us (6%)
  blocking collectives  19.1 us (4%)
  between operations  13.7 us (3%)
  other arithmetic  12.1 us (3%)
    all_gather x1, waiting for transfers between devices, local(): lax.all_gather(w_bc, 'seq', axis=0, tiled=True)  111 us
    ppermute x13, waiting for transfers between devices, passed_along(): return lax.ppermute(value, axis, pairs)  93.1 us
    ppermute x13, starting transfers between devices, passed_along(): return lax.ppermute(value, axis, pairs)  69.3 us
    reduce_scatter x1, waiting for transfers between devices, local(): lax.psum_scatter(partial_out, 'head', scatter_dimension=1, tiled=True)  50.7 us
    psum x1, blocking collectives, local(): total_sq = lax.psum(jnp.sum(gated * gated, axis=1), 'head')  19.1 us
    all_to_all x1, starting transfers between devices, local(): lax.all_to_all(jnp.stack([w_xz] * lax.axis_size('seq')), 'seq', 0, 0)  12.1 us
    unnamed x37, local copies, waits for them, and re-layouts  10 us
    another operation x1, local copies, waits for them, and re-layouts, local(): jnp.stack([w_xz] * lax.axis_size('seq'))  9.52 us
  transfers between devices with their start and end apart: 17, of which 9 were waited for; matrix products, arithmetic and copies ran while one was open for 10% of the time, Pallas kernels for 0%

profile of v1, /device:TPU:1, one launch (start us, length us, event | category | flops | bytes accessed | tf_op | source)
XLA Modules:
  0.0 433.9 jit_solution(4392044433813202755)
XLA Ops:
  6.5 9.5 %stack.2 = bf16[32,128,2,512]{3,2,1,0:T(2,128)(2,1)} broadcast(bf16[128,2,512]{2,1,0:T(2,128)(2,1)} %param.13), dimensions={1,2,3} | broadcast | bytes 8650752 | tf_op jit(solution)/shard_map/stack | solution.py:62
  16.1 12.1 %all-to-all-start = ((bf16[32,128,2,512]{3,2,1,0:T(2,128)(2,1)}), bf16[32,128,2,512]{3,2,1,0:T(2,128)(2,1)}, u32[]{:S(2)}, u32[]{:S(2)}) async-start(bf16[32,128,2,512]{3,2,1,0:T(2,128)(2,1)} %stack.2), calls=%async_computation | async-start | bytes 16777216 | tf_op jit(solution)/shard_map/all_to_all | solution.py:62
  31.8 3.6 collective-permute-start.2
  38.5 111.3 %all-gather.3.cloned.1.call-done = bf16[4096,256]{1,0:T(8,128)(2,1)} async-done(((bf16[128,256]{1,0:T(8,128)(2,1)}), bf16[4096,256]{1,0:T(8,128)(2,1)}) %all-gather.3.cloned.1.call-update) | async-done | bytes 2097168 | tf_op jit(solution)/shard_map/all_gather | solution.py:64
  149.9 4.1 convolution_convert_fusion.1
  154.0 4.8 %collective-permute-start.1 = (bf16[3,256]{1,0:T(4,128)(2,1)S(1)}, bf16[3,256]{1,0:T(4,128)(2,1)S(1)}, u32[]{:S(2)}, u32[]{:S(2)}) collective-permute-start(bf16[3,256]{1,0:T(4,128)(2,1)S(1)} %slice.154), channel_id=1, source_target_pairs={{0,8},{8,16},{16,24},{24,32},{32,40},{40,48},{48,56},{56,64},{64,7... | collective-permute-start | bytes 4616 | tf_op jit(solution)/shard_map/ppermute | solution.py:12
  159.3 70.4 %collective-permute-done.1 = bf16[3,256]{1,0:T(4,128)(2,1)S(1)} collective-permute-done((bf16[3,256]{1,0:T(4,128)(2,1)S(1)}, bf16[3,256]{1,0:T(4,128)(2,1)S(1)}, u32[]{:S(2)}, u32[]{:S(2)}) %collective-permute-start.1) | collective-permute-done | bytes 1568 | tf_op jit(solution)/shard_map/ppermute | solution.py:12
  230.1 9.3 %copy.31 = bf16[512,8,2,512]{3,1,2,0:T(8,128)(2,1)} copy(bf16[512,8,2,512]{3,2,1,0:T(2,128)(2,1)} %bitcast.35) | data formatting | bytes 16777216
  239.5 9.2 %convolution_convert_fusion = bf16[512,1024]{1,0:T(8,128)(2,1)S(1)} fusion(bf16[512,4096]{1,0:T(8,128)(2,1)} %param.12, bf16[4096,1024]{1,0:T(8,128)(2,1)} %bitcast.70), kind=kOutput, calls=%fused_computation.8 | convolution fusion | flops 4295491584 | bytes 13631488 | tf_op jit(solution)/shard_map/dot_general | solution.py:67
  248.7 3.9 collective-permute-start
  256.1 1.9 fusion.14
  258.7 3.3 collective-permute-start.7
  263.6 6.4 %collective-permute-done.7 = f32[8,64,128]{2,1,0:T(8,128)S(1)} collective-permute-done((f32[8,64,128]{2,1,0:T(8,128)S(1)}, f32[8,64,128]{2,1,0:T(8,128)S(1)}, u32[]{:S(2)}, u32[]{:S(2)}) %collective-permute-start.7) | collective-permute-done | bytes 262176 | tf_op jit(solution)/shard_map/ppermute | solution.py:12
  271.0 4.8 %collective-permute-start.8 = (f32[8,64,128]{2,1,0:T(8,128)S(1)}, f32[8,64,128]{2,1,0:T(8,128)S(1)}, u32[]{:S(2)}, u32[]{:S(2)}) collective-permute-start(f32[8,64,128]{2,1,0:T(8,128)S(1)} %broadcast_select_fusion), channel_id=1, source_target_pairs={{0,8},{8,16},{16,24},{24,32},{32,40},{40,48},{48,56},{56,64},{64,7... | collective-permute-start | bytes 786440 | tf_op jit(solution)/shard_map/ppermute | solution.py:12
  275.9 4.9 %collective-permute-start.3 = (f32[8]{0:T(128)S(1)}, f32[8]{0:T(128)S(1)}, u32[]{:S(2)}, u32[]{:S(2)}) collective-permute-start(f32[8]{0:T(128)S(1)} %broadcast_select_fusion.3), channel_id=1, source_target_pairs={{0,8},{8,16},{16,24},{24,32},{32,40},{40,48},{48,56},{56,64},{64,7... | collective-permute-start | bytes 104 | tf_op jit(solution)/shard_map/ppermute | solution.py:12
  281.8 7.8 %collective-permute-start.4 = (f32[8]{0:T(128)S(1)}, f32[8]{0:T(128)S(1)}, u32[]{:S(2)}, u32[]{:S(2)}) collective-permute-start(f32[8]{0:T(128)S(1)} %broadcast_select_fusion.4), channel_id=1, source_target_pairs={{0,16},{8,24},{16,32},{24,40},{32,48},{40,56},{48,64},{56,72},{64,... | collective-permute-start | bytes 104 | tf_op jit(solution)/shard_map/ppermute | solution.py:12
  289.7 4.3 collective-permute-start.9
  294.0 6.0 %collective-permute-start.5 = (f32[8]{0:T(128)S(1)}, f32[8]{0:T(128)S(1)}, u32[]{:S(2)}, u32[]{:S(2)}) collective-permute-start(f32[8]{0:T(128)S(1)} %broadcast_select_fusion.5), channel_id=1, source_target_pairs={{0,32},{8,40},{16,48},{24,56},{32,64},{40,72},{48,80},{56,88},{64,... | collective-permute-start | bytes 104 | tf_op jit(solution)/shard_map/ppermute | solution.py:12
  300.0 3.5 collective-permute-done.5
  303.5 9.6 %collective-permute-start.6 = (f32[8]{0:T(128)S(1)}, f32[8]{0:T(128)S(1)}, u32[]{:S(2)}, u32[]{:S(2)}) collective-permute-start(f32[8]{0:T(128)S(1)} %broadcast_select_fusion.6), channel_id=1, source_target_pairs={{0,64},{8,72},{16,80},{24,88},{32,96},{40,104},{48,112},{56,120},{... | collective-permute-start | bytes 104 | tf_op jit(solution)/shard_map/ppermute | solution.py:12
  313.2 1.3 collective-permute-start.10
  315.7 6.5 %collective-permute-done.10 = f32[8,64,128]{2,1,0:T(8,128)S(1)} collective-permute-done((f32[8,64,128]{2,1,0:T(8,128)S(1)}, f32[8,64,128]{2,1,0:T(8,128)S(1)}, u32[]{:S(2)}, u32[]{:S(2)}) %collective-permute-start.10) | collective-permute-done | bytes 262176 | tf_op jit(solution)/shard_map/ppermute | solution.py:12
  322.3 10.3 %collective-permute-start.11 = (f32[8,64,128]{2,1,0:T(8,128)S(1)}, f32[8,64,128]{2,1,0:T(8,128)S(1)}, u32[]{:S(2)}, u32[]{:S(2)}) collective-permute-start(f32[8,64,128]{2,1,0:T(8,128)S(1)} %add_select_fusion.2), channel_id=1, source_target_pairs={{0,64},{8,72},{16,80},{24,88},{32,96},{40,104},{48,112},{56,120},{... | collective-permute-start | bytes 786440 | tf_op jit(solution)/shard_map/ppermute | solution.py:12
  332.7 1.3 fusion.6
  334.0 2.4 collective-permute-done.11
  336.5 4.6 %collective-permute-start.12 = (f32[8,64,128]{2,1,0:T(8,128)S(1)}, f32[8,64,128]{2,1,0:T(8,128)S(1)}, u32[]{:S(2)}, u32[]{:S(2)}) collective-permute-start(f32[8,64,128]{2,1,0:T(8,128)S(1)} %add_select_fusion.1), channel_id=1, source_target_pairs={{0,128},{8,136},{16,144},{24,152},{32,160},{40,168},{48,176},{56,1... | collective-permute-start | bytes 786440 | tf_op jit(solution)/shard_map/ppermute | solution.py:12
  341.5 2.8 collective-permute-done.12
  345.5 2.1 multiply_reduce_fusion
  347.6 19.1 %psum.7 = f32[512]{0:T(512)S(1)} all-reduce(f32[512]{0:T(512)S(1)} %get-tuple-element.5), channel_id=1, replica_groups=mesh['seq'=32,'head'=8] {'head'}, use_global_device_ids=true, to_apply=%region_5.6 | all-reduce | flops 512 | bytes 4096 | tf_op jit(solution)/shard_map/psum | solution.py:121
  366.8 7.8 %fusion.20 = f32[512,4096]{1,0:T(8,128)} fusion(bf16[512,4096]{1,0:T(8,128)(2,1)} %all-gather.5.cloned.1.call-done, f32[512,512]{1,0:T(8,128)S(1)} %get-tuple-element.6, f32[512]{0:T(512)S(1)} %copy-done.3, f32[512]{0:T(512)S(1)} %add_rsqrt_fusion), kind=kOutput, calls=%fused_computation.36 | convolution fusion | flops 2148270080 | bytes 13635584 | tf_op jit(solution)/shard_map/dot_general | solution.py:124
  374.6 50.7 %reduce-scatter.2.cloned.1.call-done = f32[512,512]{1,0:T(8,128)} async-done(((f32[512,4096]{1,0:T(8,128)}), f32[512,512]{1,0:T(8,128)}) %reduce-scatter.2.cloned.1.call-update) | async-done | bytes 1048592 | tf_op jit(solution)/shard_map/reduce_scatter | solution.py:127
  425.3 2.1 convert_element_type.59
  (103 shorter events, 18.1 us)
Async XLA Ops:
  16.1 13.0 %copy-start.12 = (s32[512,8]{0,1:T(8,128)S(1)}, s32[512,8]{0,1:T(8,128)}, u32[]{:S(2)}) copy-start(s32[512,8]{0,1:T(8,128)} %param.19) | copy-start | bytes 49156
  16.1 21.7 %copy-start.16 = (f32[4,256]{1,0:T(4,128)S(1)}, f32[4,256]{1,0:T(4,128)}, u32[]{:S(2)}) copy-start(f32[4,256]{1,0:T(4,128)} %param.16) | copy-start | bytes 12292
  16.1 21.7 %copy-start.14 = (f32[4,512]{1,0:T(4,128)S(1)}, f32[4,512]{1,0:T(4,128)}, u32[]{:S(2)}) copy-start(f32[4,512]{1,0:T(4,128)} %param.15) | copy-start | bytes 24580
  16.1 214.1 %all-to-all-start = ((bf16[32,128,2,512]{3,2,1,0:T(2,128)(2,1)}), bf16[32,128,2,512]{3,2,1,0:T(2,128)(2,1)}, u32[]{:S(2)}, u32[]{:S(2)}) async-start(bf16[32,128,2,512]{3,2,1,0:T(2,128)(2,1)} %stack.2), calls=%async_computation | async-start | bytes 16777216 | tf_op jit(solution)/shard_map/all_to_all | solution.py:62
  28.2 121.6 %all-gather.3.cloned.1.call-start = ((), (), s32[]{:S(2)}) async-start(), calls=%async_computation.2 | async-start | bytes 2162688 | tf_op jit(solution)/shard_map/all_gather | solution.py:64
  29.0 200.8 %copy-start.17 = (bf16[3,256]{1,0:T(4,128)(2,1)S(1)}, bf16[3,256]{1,0:T(4,128)(2,1)}, u32[]{:S(2)}) copy-start(bf16[3,256]{1,0:T(4,128)(2,1)} %param.18) | copy-start | bytes 4612
  29.0 337.8 %all-gather.5.cloned.1.call-start = ((), (), s32[]{:S(2)}) async-start(), calls=%async_computation.3 | async-start | bytes 4325376 | tf_op jit(solution)/shard_map/all_gather | solution.py:125
  31.8 244.0 %collective-permute-start.2 = (f32[8]{0:T(128)}, f32[8]{0:T(128)}, u32[]{:S(2)}, u32[]{:S(2)}) collective-permute-start(f32[8]{0:T(128)} %fusion.32), channel_id=1, source_target_pairs={{0,8},{8,16},{16,24},{24,32},{32,40},{40,48},{48,56},{56,64},{64,7... | collective-permute-start | bytes 104 | tf_op jit(solution)/shard_map/ppermute | solution.py:12
  35.5 389.8 %reduce-scatter.2.cloned.1.call-start = ((), (), s32[]{:S(2)}) async-start(), calls=%async_computation.4 | async-start | bytes 9437184 | tf_op jit(solution)/shard_map/reduce_scatter | solution.py:127
  37.8 216.5 %copy-start.4 = (f32[1,512]{1,0:T(1,128)}, f32[1,512]{1,0:T(1,128)S(1)}, u32[]{:S(2)}) copy-start(f32[1,512]{1,0:T(1,128)S(1)} %get-tuple-element.15) | copy-start | bytes 6148
  37.8 216.5 %copy-start.6 = (f32[1,512]{1,0:T(1,128)}, f32[1,512]{1,0:T(1,128)S(1)}, u32[]{:S(2)}) copy-start(f32[1,512]{1,0:T(1,128)S(1)} %get-tuple-element.16) | copy-start | bytes 6148
  37.8 216.5 %copy-start.8 = (f32[1,512]{1,0:T(1,128)}, f32[1,512]{1,0:T(1,128)S(1)}, u32[]{:S(2)}) copy-start(f32[1,512]{1,0:T(1,128)S(1)} %get-tuple-element.17) | copy-start | bytes 6148
  37.8 216.5 %copy-start.10 = (f32[1,512]{1,0:T(1,128)}, f32[1,512]{1,0:T(1,128)S(1)}, u32[]{:S(2)}) copy-start(f32[1,512]{1,0:T(1,128)S(1)} %get-tuple-element.18) | copy-start | bytes 6148
  154.0 75.7 %collective-permute-start.1 = (bf16[3,256]{1,0:T(4,128)(2,1)S(1)}, bf16[3,256]{1,0:T(4,128)(2,1)S(1)}, u32[]{:S(2)}, u32[]{:S(2)}) collective-permute-start(bf16[3,256]{1,0:T(4,128)(2,1)S(1)} %slice.154), channel_id=1, source_target_pairs={{0,8},{8,16},{16,24},{24,32},{32,40},{40,48},{48,56},{56,64},{64,7... | collective-permute-start | bytes 4616 | tf_op jit(solution)/shard_map/ppermute | solution.py:12
  239.5 14.6 %copy-start.15 = (bf16[3,512]{1,0:T(4,128)(2,1)S(1)}, bf16[3,512]{1,0:T(4,128)(2,1)}, u32[]{:S(2)}) copy-start(bf16[3,512]{1,0:T(4,128)(2,1)} %param.17) | copy-start | bytes 9220
  248.7 5.4 %collective-permute-start = (bf16[3,512]{1,0:T(4,128)(2,1)S(1)}, bf16[3,512]{1,0:T(4,128)(2,1)S(1)}, u32[]{:S(2)}, u32[]{:S(2)}) collective-permute-start(bf16[3,512]{1,0:T(4,128)(2,1)S(1)} %slice.146), channel_id=1, source_target_pairs={{0,8},{8,16},{16,24},{24,32},{32,40},{40,48},{48,56},{56,64},{64,7... | collective-permute-start | bytes 9224 | tf_op jit(solution)/shard_map/ppermute | solution.py:12
  256.1 76.6 %copy-start.13 = (f32[2,8,256]{2,1,0:T(8,128)S(1)}, f32[2,8,256]{2,1,0:T(8,128)}, u32[]{:S(2)}) copy-start(f32[2,8,256]{2,1,0:T(8,128)} %get-tuple-element.10) | copy-start | bytes 49156
  258.7 11.3 %collective-permute-start.7 = (f32[8,64,128]{2,1,0:T(8,128)S(1)}, f32[8,64,128]{2,1,0:T(8,128)S(1)}, u32[]{:S(2)}, u32[]{:S(2)}) collective-permute-start(f32[8,64,128]{2,1,0:T(8,128)S(1)} %fusion.26), channel_id=1, source_target_pairs={{0,8},{8,16},{16,24},{24,32},{32,40},{40,48},{48,56},{56,64},{64,7... | collective-permute-start | bytes 786440 | tf_op jit(solution)/shard_map/ppermute | solution.py:12
  271.0 18.6 %collective-permute-start.8 = (f32[8,64,128]{2,1,0:T(8,128)S(1)}, f32[8,64,128]{2,1,0:T(8,128)S(1)}, u32[]{:S(2)}, u32[]{:S(2)}) collective-permute-start(f32[8,64,128]{2,1,0:T(8,128)S(1)} %broadcast_select_fusion), channel_id=1, source_target_pairs={{0,8},{8,16},{16,24},{24,32},{32,40},{40,48},{48,56},{56,64},{64,7... | collective-permute-start | bytes 786440 | tf_op jit(solution)/shard_map/ppermute | solution.py:12
  275.9 5.9 %collective-permute-start.3 = (f32[8]{0:T(128)S(1)}, f32[8]{0:T(128)S(1)}, u32[]{:S(2)}, u32[]{:S(2)}) collective-permute-start(f32[8]{0:T(128)S(1)} %broadcast_select_fusion.3), channel_id=1, source_target_pairs={{0,8},{8,16},{16,24},{24,32},{32,40},{40,48},{48,56},{56,64},{64,7... | collective-permute-start | bytes 104 | tf_op jit(solution)/shard_map/ppermute | solution.py:12
  281.8 12.2 %collective-permute-start.4 = (f32[8]{0:T(128)S(1)}, f32[8]{0:T(128)S(1)}, u32[]{:S(2)}, u32[]{:S(2)}) collective-permute-start(f32[8]{0:T(128)S(1)} %broadcast_select_fusion.4), channel_id=1, source_target_pairs={{0,16},{8,24},{16,32},{24,40},{32,48},{40,56},{48,64},{56,72},{64,... | collective-permute-start | bytes 104 | tf_op jit(solution)/shard_map/ppermute | solution.py:12
  289.7 23.4 %collective-permute-start.9 = (f32[8,64,128]{2,1,0:T(8,128)S(1)}, f32[8,64,128]{2,1,0:T(8,128)S(1)}, u32[]{:S(2)}, u32[]{:S(2)}) collective-permute-start(f32[8,64,128]{2,1,0:T(8,128)S(1)} %add_select_fusion.4), channel_id=1, source_target_pairs={{0,16},{8,24},{16,32},{24,40},{32,48},{40,56},{48,64},{56,72},{64,... | collective-permute-start | bytes 786440 | tf_op jit(solution)/shard_map/ppermute | solution.py:12
  294.0 9.5 %collective-permute-start.5 = (f32[8]{0:T(128)S(1)}, f32[8]{0:T(128)S(1)}, u32[]{:S(2)}, u32[]{:S(2)}) collective-permute-start(f32[8]{0:T(128)S(1)} %broadcast_select_fusion.5), channel_id=1, source_target_pairs={{0,32},{8,40},{16,48},{24,56},{32,64},{40,72},{48,80},{56,88},{64,... | collective-permute-start | bytes 104 | tf_op jit(solution)/shard_map/ppermute | solution.py:12
  303.5 11.1 %collective-permute-start.6 = (f32[8]{0:T(128)S(1)}, f32[8]{0:T(128)S(1)}, u32[]{:S(2)}, u32[]{:S(2)}) collective-permute-start(f32[8]{0:T(128)S(1)} %broadcast_select_fusion.6), channel_id=1, source_target_pairs={{0,64},{8,72},{16,80},{24,88},{32,96},{40,104},{48,112},{56,120},{... | collective-permute-start | bytes 104 | tf_op jit(solution)/shard_map/ppermute | solution.py:12
  313.2 9.0 %collective-permute-start.10 = (f32[8,64,128]{2,1,0:T(8,128)S(1)}, f32[8,64,128]{2,1,0:T(8,128)S(1)}, u32[]{:S(2)}, u32[]{:S(2)}) collective-permute-start(f32[8,64,128]{2,1,0:T(8,128)S(1)} %add_select_fusion.3), channel_id=1, source_target_pairs={{0,32},{8,40},{16,48},{24,56},{32,64},{40,72},{48,80},{56,88},{64,... | collective-permute-start | bytes 786440 | tf_op jit(solution)/shard_map/ppermute | solution.py:12
  322.3 14.0 %collective-permute-start.11 = (f32[8,64,128]{2,1,0:T(8,128)S(1)}, f32[8,64,128]{2,1,0:T(8,128)S(1)}, u32[]{:S(2)}, u32[]{:S(2)}) collective-permute-start(f32[8,64,128]{2,1,0:T(8,128)S(1)} %add_select_fusion.2), channel_id=1, source_target_pairs={{0,64},{8,72},{16,80},{24,88},{32,96},{40,104},{48,112},{56,120},{... | collective-permute-start | bytes 786440 | tf_op jit(solution)/shard_map/ppermute | solution.py:12
  332.7 11.7 %copy-start.1 = (f32[512,8]{0,1:T(8,128)S(1)}, f32[512,8]{0,1:T(8,128)}, u32[]{:S(2)}) copy-start(f32[512,8]{0,1:T(8,128)} %get-tuple-element.7) | copy-start | bytes 49156
  334.0 11.5 %copy-start.7 = (f32[1,512]{1,0:T(1,128)S(1)}, f32[1,512]{1,0:T(1,128)}, u32[]{:S(2)}) copy-start(f32[1,512]{1,0:T(1,128)} %copy-done.6) | copy-start | bytes 6148
  334.0 11.5 %copy-start.9 = (f32[1,512]{1,0:T(1,128)S(1)}, f32[1,512]{1,0:T(1,128)}, u32[]{:S(2)}) copy-start(f32[1,512]{1,0:T(1,128)} %copy-done.8) | copy-start | bytes 6148
  334.0 11.5 %copy-start.11 = (f32[1,512]{1,0:T(1,128)S(1)}, f32[1,512]{1,0:T(1,128)}, u32[]{:S(2)}) copy-start(f32[1,512]{1,0:T(1,128)} %copy-done.10) | copy-start | bytes 6148
  336.5 7.9 %collective-permute-start.12 = (f32[8,64,128]{2,1,0:T(8,128)S(1)}, f32[8,64,128]{2,1,0:T(8,128)S(1)}, u32[]{:S(2)}, u32[]{:S(2)}) collective-permute-start(f32[8,64,128]{2,1,0:T(8,128)S(1)} %add_select_fusion.1), channel_id=1, source_target_pairs={{0,128},{8,136},{16,144},{24,152},{32,160},{40,168},{48,176},{56,1... | collective-permute-start | bytes 786440 | tf_op jit(solution)/shard_map/ppermute | solution.py:12
  345.1 21.7 %copy-start.3 = (f32[512]{0:T(512)S(1)}, f32[512]{0:T(512)}, u32[]{:S(2)}) copy-start(f32[512]{0:T(512)} %param.22) | copy-start | bytes 6148
  (3 other events, 17.5 us)
Sparse Core Ops, SparseCore 0:
  31.7 118.1 all-gather.2
  152.3 136.0 all-gather.4
  374.7 50.5 reduce-scatter.1
